TPU v7x, 512 devices: a whole 4x4x16 slice. The times are simulated.
512 devices in a mesh: row: 32 (over z, core), col: 16 (over x, y).
Axes of the slice: x: 4, y: 4, z: 16, core: 2. Of those that a mesh axis runs over, the one named last changes fastest.
Arguments:
- records: float32 [9, 4096], P(None, 'row'), may hold values from -0.3 to 703, as said below
- pattern: int32 [32, 32], replicated, may hold values from 0 to 1, as said below
- iterate: float32 [4096, 4096], P('row', 'col'), may hold values from -0.5 to 0.5, as said below
Outputs:
- margin: float32 [4096, 4096], P('row', 'col')
- updated: float32 [4096, 4096], P('row', 'col')
Inputs may be any that keep to these rules, and one draw needn't show every extreme that they name: `pattern`: symmetric 0 or 1 entries; the diagonal and the first off-diagonals are 1. `records`: exponents and coefficients are positive. `iterate`: symmetric.
All inputs are finite; a program needn't handle non-finite values.
Results may differ from a plain program's by a relative error of at most 0.0003.
Values sent between devices are 32-bit elements; how exact they have to be, the bound alone decides.
No kernel may reach another device: no remote copies, remote signals or barrier semaphores. Data moves between devices by JAX's collectives and lax.ppermute only.
A program may use at most 64 MiB of HBM per device.

v0:
```python
import jax
import jax.numpy as jnp
from jax import lax
from jax.sharding import PartitionSpec as P

BLOCK = 128
PRIMS = 3


def expand(blocks, size):
    row_blocks, col_blocks = blocks.shape
    grown = jnp.broadcast_to(blocks[:, None, :, None], (row_blocks, size, col_blocks, size))
    return grown.reshape(row_blocks * size, col_blocks * size).astype(jnp.float32)


def pair_margin(left, right):
    distance = (left[0][:, None] - right[0][None, :]) ** 2
    distance = distance + (left[1][:, None] - right[1][None, :]) ** 2
    distance = distance + (left[2][:, None] - right[2][None, :]) ** 2
    accumulated = jnp.zeros(distance.shape, jnp.float32)
    for p in range(PRIMS):
        for q in range(PRIMS):
            exponent_a = left[3 + p][:, None]
            exponent_b = right[3 + q][None, :]
            summed = exponent_a + exponent_b
            prefactor = (2.0 * jnp.sqrt(exponent_a * exponent_b) / summed) ** 1.5
            weight_ab = left[3 + PRIMS + p][:, None] * right[3 + PRIMS + q][None, :]
            accumulated = accumulated + weight_ab * prefactor * jnp.exp(
                -(exponent_a * exponent_b / summed) * distance
            )
    return accumulated


def self_norm(recs):
    accumulated = jnp.zeros(recs.shape[1], jnp.float32)
    for p in range(PRIMS):
        for q in range(PRIMS):
            exponent_a = recs[3 + p]
            exponent_b = recs[3 + q]
            prefactor = (2.0 * jnp.sqrt(exponent_a * exponent_b) / (exponent_a + exponent_b)) ** 1.5
            accumulated = accumulated + recs[3 + PRIMS + p] * recs[3 + PRIMS + q] * prefactor
    return accumulated


def matmul(left, right):
    return jnp.dot(left, right, precision=lax.Precision.HIGHEST, preferred_element_type=jnp.float32)


def accumulate(left, piece):
    return matmul(left, piece)


def body(records, pattern, iterate):
    row_idx = lax.axis_index("row")
    col_idx = lax.axis_index("col")
    row_count, col_count = iterate.shape
    row_blocks = row_count // BLOCK
    col_blocks = col_count // BLOCK
    everyone = lax.all_gather(records, "row", axis=1, tiled=True)
    col_records = lax.dynamic_slice_in_dim(everyone, col_idx * col_count, col_count, 1)
    row_norms = self_norm(records)
    col_norms = self_norm(col_records)
    tile_blocks = lax.dynamic_slice(
        pattern, (row_idx * row_blocks, col_idx * col_blocks), (row_blocks, col_blocks)
    )
    tile_mask = expand(tile_blocks, BLOCK)
    margin = tile_mask * (
        pair_margin(records, col_records) / jnp.sqrt(row_norms[:, None] * col_norms[None, :])
    )
    masked = tile_mask * iterate
    margin_row = lax.all_gather(margin, "col", axis=1, tiled=True)
    iterate_row = lax.all_gather(masked, "col", axis=1, tiled=True)
    iterate_col = lax.all_gather(masked, "row", axis=0, tiled=True)
    product_one = tile_mask * matmul(margin_row, iterate_col)
    product_two = tile_mask * accumulate(
        iterate_row, lax.all_gather(product_one, "row", axis=0, tiled=True)
    )
    second_row = lax.all_gather(product_two, "col", axis=1, tiled=True)
    product_three = matmul(second_row, iterate_col)
    updated = tile_mask * (1.5 * masked - 0.5 * product_three)
    return (margin, updated)


def solution(mesh):
    in_specs = (P(None, "row"), P(), P("row", "col"))
    out_specs = (P("row", "col"), P("row", "col"))
    return jax.shard_map(body, mesh=mesh, in_specs=in_specs, out_specs=out_specs, check_vma=False)
```

profile of v0, /device:TPU:2, one launch (start us, length us, event | category | flops | bytes accessed | tf_op | source)
XLA Modules:
  0.0 397.7 jit_solution(15753159277731944957)
XLA Ops:
  7.2 0.0 copy-start
  7.2 0.0 all-gather.8.cloned.1.call-start
  7.2 0.9 multiply_add_fusion.1
  8.1 1.0 slice_bitcast_fusion.8
  9.1 37.2 %all_gather.18 = f32[9,4096]{1,0:T(8,128)S(1)} all-gather(f32[9,128]{1,0:T(8,128)} %param.3), channel_id=1, replica_groups=mesh['row'=32,'col'=16] {'row'}, dimensions={1}, use_global_device_ids=true | all-gather | bytes 152064 | tf_op jit(solution)/shard_map/all_gather | solution.py:59
  46.3 0.8 convert_bitcast_fusion
  47.1 0.1 broadcast_bitcast_fusion
  47.1 0.1 constant_dynamic-slice_fusion
  47.3 2.1 fusion.74
  49.4 0.0 all-gather.8.cloned.1.call-update
  49.4 0.0 all-gather.10.cloned.1.call-start
  49.5 0.0 copy-done
  49.5 0.7 broadcast_multiply_fusion
  50.2 0.0 all-gather.10.cloned.1.call-update
  50.2 0.0 all-gather.6.cloned.1.call-start
  50.3 0.7 all-gather.6.cloned.1.call-update
  50.9 0.0 all-gather.12.cloned.1.call-start
  51.0 56.6 %all-gather.8.cloned.1.call-done = f32[128,4096]{1,0:T(8,128)} async-done(((f32[128,256]{1,0:T(8,128)}), f32[128,4096]{1,0:T(8,128)}) %all-gather.8.cloned.1.call-update) | async-done | bytes 2097168 | tf_op jit(solution)/shard_map/all_gather | solution.py:71
  107.6 75.9 %all-gather.10.cloned.1.call-done = f32[4096,256]{1,0:T(8,128)} async-done(((f32[128,256]{1,0:T(8,128)}), f32[4096,256]{1,0:T(8,128)}) %all-gather.10.cloned.1.call-update) | async-done | bytes 4194320 | tf_op jit(solution)/shard_map/all_gather | solution.py:73
  183.4 5.6 %convolution_multiply_fusion.2 = f32[128,256]{1,0:T(8,128)} fusion(f32[128,4096]{1,0:T(8,128)} %all-gather.8.cloned.1.call-done, f32[4096,256]{1,0:T(8,128)} %all-gather.10.cloned.1.call-done, f32[256]{0:T(256)S(1)} %broadcast_bitcast_fusion), kind=kOutput, calls=%fused_computation.4 | convolution fusion | flops 1610645504 | bytes 6423552 | tf_op jit(solution)/shard_map/dot_general | solution.py:46
  189.0 0.0 all-gather.12.cloned.1.call-update
  189.1 0.0 all-gather.14.cloned.1.call-start
  189.1 56.8 %all-gather.6.cloned.1.call-done = f32[128,4096]{1,0:T(8,128)} async-done(((f32[128,256]{1,0:T(8,128)}), f32[128,4096]{1,0:T(8,128)}) %all-gather.6.cloned.1.call-update) | async-done | bytes 2097168 | tf_op jit(solution)/shard_map/all_gather | solution.py:72
  245.9 75.1 %all-gather.12.cloned.1.call-done = f32[4096,256]{1,0:T(8,128)} async-done(((f32[128,256]{1,0:T(8,128)}), f32[4096,256]{1,0:T(8,128)}) %all-gather.12.cloned.1.call-update) | async-done | bytes 4194320 | tf_op jit(solution)/shard_map/all_gather | solution.py:76
  321.0 5.6 %convolution_multiply_fusion.1 = f32[128,256]{1,0:T(8,128)} fusion(f32[128,4096]{1,0:T(8,128)} %all-gather.6.cloned.1.call-done, f32[4096,256]{1,0:T(8,128)} %all-gather.12.cloned.1.call-done, f32[256]{0:T(256)S(1)} %broadcast_bitcast_fusion), kind=kOutput, calls=%fused_computation.3 | convolution fusion | flops 1610645504 | bytes 6423552 | tf_op jit(solution)/shard_map/dot_general | solution.py:46
  326.6 0.0 all-gather.14.cloned.1.call-update
  326.6 59.0 %all-gather.14.cloned.1.call-done = f32[128,4096]{1,0:T(8,128)} async-done(((f32[128,256]{1,0:T(8,128)}), f32[128,4096]{1,0:T(8,128)}) %all-gather.14.cloned.1.call-update) | async-done | bytes 2097168 | tf_op jit(solution)/shard_map/all_gather | solution.py:78
  385.6 5.6 %fusion.1 = f32[128,256]{1,0:T(8,128)} fusion(f32[128,4096]{1,0:T(8,128)} %all-gather.14.cloned.1.call-done, f32[4096,256]{1,0:T(8,128)} %all-gather.10.cloned.1.call-done, f32[256]{0:T(256)S(1)} %broadcast_bitcast_fusion, f32[128,256]{1,0:T(8,128)S(1)} %copy-done), kind=kOutput, calls=%fused_computation.2 | convolution fusion | flops 1610776576 | bytes 6554624 | tf_op jit(solution)/shard_map/dot_general | solution.py:46
Async XLA Ops:
  7.2 42.3 %copy-start = (f32[128,256]{1,0:T(8,128)S(1)}, f32[128,256]{1,0:T(8,128)}, u32[]{:S(2)}) copy-start(f32[128,256]{1,0:T(8,128)} %param.5) | copy-start | bytes 393220
  7.2 100.4 %all-gather.8.cloned.1.call-start = ((), (), s32[]{:S(2)}) async-start(), calls=%async_computation.1 | async-start | bytes 2228224 | tf_op jit(solution)/shard_map/all_gather | solution.py:71
  49.4 134.0 %all-gather.10.cloned.1.call-start = ((), (), s32[]{:S(2)}) async-start(), calls=%async_computation.2 | async-start | bytes 4325376 | tf_op jit(solution)/shard_map/all_gather | solution.py:73
  50.2 195.7 %all-gather.6.cloned.1.call-start = ((), (), s32[]{:S(2)}) async-start(), calls=%async_computation | async-start | bytes 2228224 | tf_op jit(solution)/shard_map/all_gather | solution.py:72
  50.9 270.1 %all-gather.12.cloned.1.call-start = ((), (), s32[]{:S(2)}) async-start(), calls=%async_computation.3 | async-start | bytes 4325376 | tf_op jit(solution)/shard_map/all_gather | solution.py:76
  189.1 196.6 %all-gather.14.cloned.1.call-start = ((), (), s32[]{:S(2)}) async-start(), calls=%async_computation.4 | async-start | bytes 2228224 | tf_op jit(solution)/shard_map/all_gather | solution.py:78
Sparse Core Ops, SparseCore 0:
  49.6 57.9 all-gather.7
  110.3 73.1 all-gather.9
  187.0 58.8 all-gather.5
  247.9 73.1 all-gather.11
  326.8 58.8 all-gather.13
where the time goes:
time: 398 us
  waiting for transfers between devices  324 us (81%)
  blocking collectives  37.2 us (9%)
  matrix products  16.7 us (4%)
  between operations  13.8 us (3%)
  other arithmetic  4.61 us (1%)
    all_gather x1, waiting for transfers between devices, body(): iterate_col = lax.all_gather(masked, 'row', axis=0, tiled=True)  75.9 us
    all_gather x1, waiting for transfers between devices, body(): lax.all_gather(product_one, 'row', axis=0, tiled=True)  75.1 us
    all_gather x1, waiting for transfers between devices, body(): second_row = lax.all_gather(product_two, 'col', axis=1, tiled=True)  59 us
    all_gather x1, waiting for transfers between devices, body(): iterate_row = lax.all_gather(masked, 'col', axis=1, tiled=True)  56.8 us
    all_gather x1, waiting for transfers between devices, body(): margin_row = lax.all_gather(margin, 'col', axis=1, tiled=True)  56.6 us
    all_gather x1, blocking collectives, body(): everyone = lax.all_gather(records, 'row', axis=1, tiled=True)  37.2 us
    dot_general x3, matrix products, matmul(): jnp.dot(left, right, precision=lax.Precision.HIGHEST, preferred_element_t...  16.7 us
  transfers between devices with their start and end apart: 5, of which 5 were waited for; matrix products, arithmetic and copies ran while one was open for 2% of the time, Pallas kernels for 0%

commit v1 on v0

--- a/solution.py
+++ b/solution.py
@@ -70,7 +70,10 @@
     masked = tile_mask * iterate
     margin_row = lax.all_gather(margin, "col", axis=1, tiled=True)
     iterate_row = lax.all_gather(masked, "col", axis=1, tiled=True)
-    iterate_col = lax.all_gather(masked, "row", axis=0, tiled=True)
+    count = lax.axis_size("row")
+    parts = jnp.stack([masked for _ in range(count)])
+    parts = lax.all_to_all(parts, "row", split_axis=0, concat_axis=0)
+    iterate_col = jnp.concatenate(parts, axis=0)
     product_one = tile_mask * matmul(margin_row, iterate_col)
     product_two = tile_mask * accumulate(
         iterate_row, lax.all_gather(product_one, "row", axis=0, tiled=True)

time: 398 us -> 516 us (1.30)
  blocking collectives: 37.2 us -> 207 us
  waiting for transfers between devices: 324 us -> 255 us
  starting transfers between devices: 0.2 us -> 15.9 us
    all_gather x1, blocking collectives: 37.2 us -> 207 us  [body(): everyone = lax.all_gather(records, 'row', axis=1, tiled=True)]
    all_gather x1 -> x0, waiting for transfers between devices: 75.9 us -> none  [body(): iterate_col = lax.all_gather(masked, 'row', axis=0, tiled=True)]
    all_to_all x0 -> x1, starting transfers between devices: none -> 15.7 us  [body(): parts = lax.all_to_all(parts, 'row', split_axis=0, concat_axis=0)]
  transfers between devices with their start and end apart: 5 -> 5, of which waited for: 5 -> 4; matrix products, arithmetic and copies ran while one was open for 2% -> 2% of each run, Pallas kernels for 0% -> 0%
where the time goes in v1:
time: 516 us
  waiting for transfers between devices  255 us (49%)
  blocking collectives  207 us (40%)
  matrix products  16.7 us (3%)
  starting transfers between devices  15.9 us (3%)
  between operations  13.8 us (3%)
    all_gather x1, blocking collectives, body(): everyone = lax.all_gather(records, 'row', axis=1, tiled=True)  207 us
    all_gather x1, waiting for transfers between devices, body(): lax.all_gather(product_one, 'row', axis=0, tiled=True)  75.3 us
    all_gather x1, waiting for transfers between devices, body(): margin_row = lax.all_gather(margin, 'col', axis=1, tiled=True)  60.7 us
    all_gather x1, waiting for transfers between devices, body(): iterate_row = lax.all_gather(masked, 'col', axis=1, tiled=True)  59.7 us
    all_gather x1, waiting for transfers between devices, body(): second_row = lax.all_gather(product_two, 'col', axis=1, tiled=True)  59 us
    dot_general x3, matrix products, matmul(): jnp.dot(left, right, precision=lax.Precision.HIGHEST, preferred_element_t...  16.7 us
    all_to_all x1, starting transfers between devices, body(): parts = lax.all_to_all(parts, 'row', split_axis=0, concat_axis=0)  15.7 us
  transfers between devices with their start and end apart: 5, of which 4 were waited for; matrix products, arithmetic and copies ran while one was open for 2% of the time, Pallas kernels for 0%

profile of v1, /device:TPU:2, one launch (start us, length us, event | category | flops | bytes accessed | tf_op | source)
XLA Modules:
  0.0 515.8 jit_solution(10527452703363746720)
XLA Ops:
  7.2 0.8 convert_bitcast_fusion
  7.9 0.1 broadcast_bitcast_fusion
  8.0 0.9 broadcast_multiply_fusion
  8.9 0.0 copy-start
  8.9 2.5 stack.2
  11.4 0.0 copy-start.2
  11.4 0.0 copy-done
  11.4 15.7 %all-to-all-start = ((f32[32,128,256]{2,1,0:T(8,128)}), f32[32,128,256]{2,1,0:T(8,128)}, u32[]{:S(2)}, u32[]{:S(2)}) async-start(f32[32,128,256]{2,1,0:T(8,128)} %stack.2), calls=%async_computation | async-start | bytes 8388608 | tf_op jit(solution)/shard_map/all_to_all | solution.py:75
  27.2 0.0 all-gather.7.cloned.1.call-start
  27.2 0.0 copy-done.2
  27.2 207.4 %all_gather.15 = f32[9,4096]{1,0:T(8,128)S(1)} all-gather(f32[9,128]{1,0:T(8,128)S(1)} %copy-done.2), channel_id=1, replica_groups=mesh['row'=32,'col'=16] {'row'}, dimensions={1}, use_global_device_ids=true | all-gather | bytes 152064 | tf_op jit(solution)/shard_map/all_gather | solution.py:59
  234.6 0.1 constant_dynamic-slice_fusion
  234.8 2.1 fusion.74
  237.0 0.0 all-gather.7.cloned.1.call-update
  237.0 0.0 all-gather.5.cloned.1.call-start
  237.0 0.7 all-gather.5.cloned.1.call-update
  237.7 0.0 all-gather.9.cloned.1.call-start
  237.8 60.7 %all-gather.7.cloned.1.call-done = f32[128,4096]{1,0:T(8,128)} async-done(((f32[128,256]{1,0:T(8,128)}), f32[128,4096]{1,0:T(8,128)}) %all-gather.7.cloned.1.call-update) | async-done | bytes 2097168 | tf_op jit(solution)/shard_map/all_gather | solution.py:71
  298.5 0.0 all-to-all-done
  298.5 5.6 %convolution_multiply_fusion.2 = f32[128,256]{1,0:T(8,128)} fusion(f32[128,4096]{1,0:T(8,128)} %all-gather.7.cloned.1.call-done, f32[4096,256]{1,0:T(8,128)} %bitcast.21, f32[256]{0:T(256)S(1)} %broadcast_bitcast_fusion), kind=kOutput, calls=%fused_computation.4 | convolution fusion | flops 1610645504 | bytes 6423552 | tf_op jit(solution)/shard_map/dot_general | solution.py:46
  304.0 0.0 copy-start.1
  304.0 0.0 all-gather.9.cloned.1.call-update
  304.1 0.0 all-gather.11.cloned.1.call-start
  304.1 59.7 %all-gather.5.cloned.1.call-done = f32[128,4096]{1,0:T(8,128)} async-done(((f32[128,256]{1,0:T(8,128)}), f32[128,4096]{1,0:T(8,128)}) %all-gather.5.cloned.1.call-update) | async-done | bytes 2097168 | tf_op jit(solution)/shard_map/all_gather | solution.py:72
  363.9 75.3 %all-gather.9.cloned.1.call-done = f32[4096,256]{1,0:T(8,128)} async-done(((f32[128,256]{1,0:T(8,128)}), f32[4096,256]{1,0:T(8,128)}) %all-gather.9.cloned.1.call-update) | async-done | bytes 4194320 | tf_op jit(solution)/shard_map/all_gather | solution.py:79
  439.2 5.6 %convolution_multiply_fusion.1 = f32[128,256]{1,0:T(8,128)} fusion(f32[128,4096]{1,0:T(8,128)} %all-gather.5.cloned.1.call-done, f32[4096,256]{1,0:T(8,128)} %all-gather.9.cloned.1.call-done, f32[256]{0:T(256)S(1)} %broadcast_bitcast_fusion), kind=kOutput, calls=%fused_computation.3 | convolution fusion | flops 1610645504 | bytes 6423552 | tf_op jit(solution)/shard_map/dot_general | solution.py:46
  444.7 0.0 all-gather.11.cloned.1.call-update
  444.8 59.0 %all-gather.11.cloned.1.call-done = f32[128,4096]{1,0:T(8,128)} async-done(((f32[128,256]{1,0:T(8,128)}), f32[128,4096]{1,0:T(8,128)}) %all-gather.11.cloned.1.call-update) | async-done | bytes 2097168 | tf_op jit(solution)/shard_map/all_gather | solution.py:81
  503.7 0.0 copy-done.1
  503.7 5.6 %fusion.1 = f32[128,256]{1,0:T(8,128)} fusion(f32[128,4096]{1,0:T(8,128)} %all-gather.11.cloned.1.call-done, f32[4096,256]{1,0:T(8,128)} %bitcast.21, f32[256]{0:T(256)S(1)} %broadcast_bitcast_fusion, f32[128,256]{1,0:T(8,128)S(1)} %copy-done.1), kind=kOutput, calls=%fused_computation.2 | convolution fusion | flops 1610776576 | bytes 6554624 | tf_op jit(solution)/shard_map/dot_general | solution.py:46
  (2 shorter events, 0.0 us)
Async XLA Ops:
  8.9 2.5 copy-start
  11.4 15.8 %copy-start.2 = (f32[9,128]{1,0:T(8,128)S(1)}, f32[9,128]{1,0:T(8,128)}, u32[]{:S(2)}) copy-start(f32[9,128]{1,0:T(8,128)} %param.3) | copy-start | bytes 13828
  11.4 287.1 %all-to-all-start = ((f32[32,128,256]{2,1,0:T(8,128)}), f32[32,128,256]{2,1,0:T(8,128)}, u32[]{:S(2)}, u32[]{:S(2)}) async-start(f32[32,128,256]{2,1,0:T(8,128)} %stack.2), calls=%async_computation | async-start | bytes 8388608 | tf_op jit(solution)/shard_map/all_to_all | solution.py:75
  27.2 271.3 %all-gather.7.cloned.1.call-start = ((), (), s32[]{:S(2)}) async-start(), calls=%async_computation.2 | async-start | bytes 2228224 | tf_op jit(solution)/shard_map/all_gather | solution.py:71
  237.0 126.9 %all-gather.5.cloned.1.call-start = ((), (), s32[]{:S(2)}) async-start(), calls=%async_computation.1 | async-start | bytes 2228224 | tf_op jit(solution)/shard_map/all_gather | solution.py:72
  237.7 201.4 %all-gather.9.cloned.1.call-start = ((), (), s32[]{:S(2)}) async-start(), calls=%async_computation.3 | async-start | bytes 4325376 | tf_op jit(solution)/shard_map/all_gather | solution.py:79
  304.0 199.7 %copy-start.1 = (f32[128,256]{1,0:T(8,128)S(1)}, f32[128,256]{1,0:T(8,128)}, u32[]{:S(2)}) copy-start(f32[128,256]{1,0:T(8,128)} %param.5) | copy-start | bytes 393220
  304.1 199.7 %all-gather.11.cloned.1.call-start = ((), (), s32[]{:S(2)}) async-start(), calls=%async_computation.4 | async-start | bytes 2228224 | tf_op jit(solution)/shard_map/all_gather | solution.py:81
Sparse Core Ops, SparseCore 0:
  237.1 61.2 all-gather.6
  302.0 61.7 all-gather.4
  366.0 73.1 all-gather.8
  444.9 58.8 all-gather.10
